TPU v7x, 32 devices: a whole 2x2x4 slice. The times are simulated.
32 devices in a mesh: dp: 8 (over y, x, core), img: 4 (over z).
Axes of the slice: x: 2, y: 2, z: 4, core: 2. Of those that a mesh axis runs over, the one named last changes fastest.
Arguments:
- tokens: bfloat16 [256, 64, 768], P(('dp', 'img')), may hold values from -3 to 3
- image_tokens: bfloat16 [256, 256, 768], P('dp', 'img'), may hold values from -4 to 4
- token_counts: int32 [256], P('dp'), may hold values from 1 to 256, 40960 in all
- self_qkv: bfloat16 [768, 2304], P('dp', 'img'), may hold values from -0.21875 to 0.21875
- self_out: bfloat16 [768, 768], P('dp', 'img'), may hold values from -0.4375 to 0.4375
- cross_q: bfloat16 [768, 768], P('dp', 'img'), may hold values from -0.21875 to 0.21875
- cross_kv: bfloat16 [768, 1536], P('dp', 'img'), may hold values from -0.21875 to 0.21875
- cross_out: bfloat16 [768, 768], P('dp', 'img'), may hold values from -0.625 to 0.625
- mlp_in: bfloat16 [768, 3072], P('dp', 'img'), may hold values from -0.21875 to 0.21875
- mlp_out: bfloat16 [3072, 768], P('dp', 'img'), may hold values from -0.109375 to 0.109375
- norm_gains: float32 [3, 768], P(None, 'dp'), may hold values from 0.25 to 1.75
- shifts: float32 [10, 768], P(None, 'dp'), may hold values from -1 to 1
- mlp_bias: float32 [3072], P('dp'), may hold values from -1 to 1
- cotangent: bfloat16 [256, 64, 768], P(('dp', 'img')), may hold values from -8 to 8
Outputs:
- layer_out: bfloat16 [256, 64, 768], P(('dp', 'img'))
- token_grads: bfloat16 [256, 64, 768], P(('dp', 'img'))
- image_grads: bfloat16 [256, 256, 768], P('dp', 'img')
- g_self_qkv: float32 [768, 2304], P('dp', 'img')
- g_self_out: float32 [768, 768], P('dp', 'img')
- g_cross_q: float32 [768, 768], P('dp', 'img')
- g_cross_kv: float32 [768, 1536], P('dp', 'img')
- g_cross_out: float32 [768, 768], P('dp', 'img')
- g_mlp_in: float32 [768, 3072], P('dp', 'img')
- g_mlp_out: float32 [3072, 768], P('dp', 'img')
- g_norm_gains: float32 [3, 768], P(None, 'dp')
- g_shifts: float32 [10, 768], P(None, 'dp')
- g_mlp_bias: float32 [3072], P('dp')
Inputs may be any that keep to these rules, and one draw needn't show every extreme that they name: The first token_counts[c] pooled tokens of caption c's image are valid; some image has all 256 valid.
All inputs are finite; a program needn't handle non-finite values. No bound on the sum of `token_counts` on one device may be relied on, other than what follows from the above.
Results may differ from a plain program's by a relative error of at most 0.03.
Values may be sent and summed in bfloat16 or wider, within the bound.
A program may use at most 192 MiB of HBM per device.

v0:
```python
import jax
import jax.numpy as jnp
from jax import lax
from jax.sharding import PartitionSpec as P

MODEL_WIDTH = 768
HEADS = 12
HEAD = 64
SEQ = 64


masked_value = -1e30
norm_epsilon = 1e-05


def joined(value, axis, combine):
    everything = jax.tree.map(lambda part: lax.all_gather(part, axis), value)
    first = jax.tree.map(lambda part: part[0], everything)

    def hop(k, so_far):
        return combine(so_far, jax.tree.map(lambda part: part[k], everything))

    return lax.fori_loop(1, lax.axis_size(axis), hop, first)


def layer_norm(values, norm_gain, norm_shift):
    average = jnp.mean(values, axis=-1, keepdims=True)
    centred = values - average
    spread = jnp.mean(centred * centred, axis=-1, keepdims=True)
    return centred * lax.rsqrt(spread + norm_epsilon) * norm_gain + norm_shift


def matmul(left_op, right_op):
    return jnp.dot(left_op, right_op, preferred_element_type=jnp.float32)


def matmul_tleft(left_op, right_op):
    return lax.dot_general(
        left_op, right_op, (((0,), (0,)), ((), ())), preferred_element_type=jnp.float32
    )


def matmul_tright(left_op, right_op):
    return lax.dot_general(
        left_op, right_op, (((1,), (1,)), ((), ())), preferred_element_type=jnp.float32
    )


def column_sums(values):
    return jnp.sum(values.astype(jnp.float32), axis=0)


def to_heads(values, pair_count):
    return values.reshape(pair_count, -1, HEADS, HEAD)


def self_allowed():
    places = jnp.arange(2 * SEQ, dtype=jnp.int32)
    same_caption = places[:, None] // SEQ == places[None, :] // SEQ
    return (same_caption & (places[None, :] <= places[:, None]))[None, None]


def cross_allowed(token_counts, block_len):
    pair_count = token_counts.shape[0] // 2
    query_image = jnp.arange(2 * SEQ, dtype=jnp.int32) // SEQ
    key_places = jnp.arange(2 * block_len, dtype=jnp.int32)
    key_image = key_places // block_len
    key_index = lax.axis_index("img") * block_len + key_places % block_len
    paired = token_counts.reshape(pair_count, 2)
    key_limit = jnp.where(key_image[None, :] == 0, paired[:, 0:1], paired[:, 1:2])
    valid_keys = key_index[None, :] < key_limit
    same_image = query_image[:, None] == key_image[None, :]
    return (same_image[None] & valid_keys[:, None, :])[:, None]


def head_scores(queries, key_heads, allowed):
    scores = jnp.einsum(
        "pqhd,pkhd->phqk", queries, key_heads, preferred_element_type=jnp.float32
    ) * HEAD ** (-0.5)
    return jnp.where(allowed, scores, masked_value)


def attend_grads(grad_scores, attn_probs, queries, key_heads, grad_mixed):
    score_scale = HEAD ** (-0.5)
    grad_queries = (
        jnp.einsum("phqk,pkhd->pqhd", grad_scores, key_heads, preferred_element_type=jnp.float32)
        * score_scale
    )
    grad_keys = (
        jnp.einsum("phqk,pqhd->pkhd", grad_scores, queries, preferred_element_type=jnp.float32)
        * score_scale
    )
    grad_values = jnp.einsum(
        "phqk,pqhd->pkhd",
        attn_probs.astype(jnp.bfloat16),
        grad_mixed,
        preferred_element_type=jnp.float32,
    )
    return (grad_queries, grad_keys.astype(jnp.bfloat16), grad_values.astype(jnp.bfloat16))


def self_forward(queries, key_heads, value_heads, allowed):
    scores = head_scores(queries, key_heads, allowed)
    top_score = jnp.max(scores, axis=-1, keepdims=True)
    weights = jnp.exp(scores - top_score)
    totals = jnp.sum(weights, axis=-1, keepdims=True)
    attn_probs = (weights / totals).astype(jnp.bfloat16)
    mixed_heads = jnp.einsum(
        "phqk,pkhd->pqhd", attn_probs, value_heads, preferred_element_type=jnp.float32
    )
    return (mixed_heads, top_score + jnp.log(totals))


def self_attention_backward(queries, key_heads, value_heads, allowed, log_totals, grad_mixed):
    scores = head_scores(queries, key_heads, allowed)
    attn_probs = jnp.exp(scores - log_totals)
    grad_probs = jnp.einsum(
        "pqhd,pkhd->phqk", grad_mixed, value_heads, preferred_element_type=jnp.float32
    )
    inner_term = jnp.sum(attn_probs * grad_probs, axis=-1, keepdims=True)
    grad_scores = (attn_probs * (grad_probs - inner_term)).astype(jnp.bfloat16)
    return attend_grads(grad_scores, attn_probs, queries, key_heads, grad_mixed)


def merge_totals(earlier, later):
    top_score = jnp.maximum(earlier[0], later[0])
    return (
        top_score,
        earlier[1] * jnp.exp(earlier[0] - top_score) + later[1] * jnp.exp(later[0] - top_score),
    )


def cross_forward(queries, key_heads, value_heads, allowed):
    scores = head_scores(queries, key_heads, allowed)
    local_top = jnp.max(scores, axis=-1)
    local_total = jnp.sum(jnp.where(allowed, jnp.exp(scores - local_top[..., None]), 0.0), axis=-1)
    top_score, total_sum = joined((local_top, local_total), "img", merge_totals)
    attn_probs = (jnp.exp(scores - top_score[..., None]) / total_sum[..., None]).astype(
        jnp.bfloat16
    )
    partial_mixed = jnp.einsum(
        "phqk,pkhd->pqhd", attn_probs, value_heads, preferred_element_type=jnp.float32
    )
    return (partial_mixed, top_score, total_sum)


def cross_backward(queries, key_heads, value_heads, allowed, top_score, total_sum, grad_mixed):
    scores = head_scores(queries, key_heads, allowed)
    attn_probs = jnp.exp(scores - top_score[..., None]) / total_sum[..., None]
    grad_probs = jnp.einsum(
        "pqhd,pkhd->phqk", grad_mixed, value_heads, preferred_element_type=jnp.float32
    )
    local_inner = jnp.sum(attn_probs * grad_probs, axis=-1)
    inner_term = lax.psum(local_inner, "img")
    grad_scores = (attn_probs * (grad_probs - inner_term[..., None])).astype(jnp.bfloat16)
    return attend_grads(grad_scores, attn_probs, queries, key_heads, grad_mixed)


def local(
    tokens,
    image_tokens,
    token_counts,
    self_qkv,
    self_out,
    cross_q,
    cross_kv,
    cross_out,
    mlp_in,
    mlp_out,
    norm_gains,
    shifts,
    mlp_bias,
    cotangent,
):
    wide_parts = (
        lax.all_gather(self_qkv, "img", axis=1, tiled=True),
        lax.all_gather(self_out, "img", axis=1, tiled=True),
        lax.all_gather(cross_q, "img", axis=1, tiled=True),
        lax.all_gather(cross_kv, "img", axis=1, tiled=True),
        lax.all_gather(cross_out, "img", axis=1, tiled=True),
        lax.all_gather(mlp_in, "img", axis=1, tiled=True),
        lax.all_gather(mlp_out, "img", axis=1, tiled=True),
    )
    all_params = (
        lax.all_gather(wide_parts[0], "dp", axis=0, tiled=True),
        lax.all_gather(wide_parts[1], "dp", axis=0, tiled=True),
        lax.all_gather(wide_parts[2], "dp", axis=0, tiled=True),
        lax.all_gather(wide_parts[3], "dp", axis=0, tiled=True),
        lax.all_gather(wide_parts[4], "dp", axis=0, tiled=True),
        lax.all_gather(wide_parts[5], "dp", axis=0, tiled=True),
        lax.all_gather(wide_parts[6], "dp", axis=0, tiled=True),
        lax.all_gather(norm_gains.astype(jnp.bfloat16), "dp", axis=1, tiled=True).astype(
            norm_gains.dtype
        ),
        lax.all_gather(shifts.astype(jnp.bfloat16), "dp", axis=1, tiled=True).astype(shifts.dtype),
        lax.all_gather(mlp_bias.astype(jnp.bfloat16), "dp", axis=0, tiled=True).astype(
            mlp_bias.dtype
        ),
    )
    qkv_w, sout_w, cq_w, ckv_w, cout_w, in_w, outm_w, gain_rows, shift_rows, inner_bias = all_params
    captions = tokens.shape[0]
    total_row_count = captions * SEQ
    pair_count = captions // 2
    group_caps = image_tokens.shape[0]
    group_pairs = group_caps // 2
    block_len = image_tokens.shape[1]
    zero_row = jnp.zeros((MODEL_WIDTH,), jnp.float32)
    rows = tokens.reshape(total_row_count, MODEL_WIDTH).astype(jnp.float32)
    normed1 = layer_norm(rows, gain_rows[0], shift_rows[0]).astype(jnp.bfloat16)
    mixed_qkv = (
        matmul(normed1, qkv_w) + jnp.concatenate([shift_rows[3], zero_row, shift_rows[4]])
    ).astype(jnp.bfloat16)
    self_queries = to_heads(mixed_qkv[:, :MODEL_WIDTH], pair_count)
    self_keys = to_heads(mixed_qkv[:, MODEL_WIDTH : 2 * MODEL_WIDTH], pair_count)
    self_values = to_heads(mixed_qkv[:, 2 * MODEL_WIDTH :], pair_count)
    causal = self_allowed()
    self_mixed, self_logs = self_forward(self_queries, self_keys, self_values, causal)
    self_mixed = self_mixed.reshape(total_row_count, MODEL_WIDTH).astype(jnp.bfloat16)
    first_sum = rows + matmul(self_mixed, sout_w) + shift_rows[5]
    normed2 = layer_norm(first_sum, gain_rows[1], shift_rows[1]).astype(jnp.bfloat16)
    cross_query = (matmul(normed2, cq_w) + shift_rows[6]).astype(jnp.bfloat16)
    group_queries = to_heads(lax.all_gather(cross_query, "img", axis=0, tiled=True), group_pairs)
    image_rows = image_tokens.reshape(group_caps * block_len, MODEL_WIDTH)
    image_kv = (matmul(image_rows, ckv_w) + jnp.concatenate([zero_row, shift_rows[7]])).astype(
        jnp.bfloat16
    )
    cross_keys = to_heads(image_kv[:, :MODEL_WIDTH], group_pairs)
    cross_values = to_heads(image_kv[:, MODEL_WIDTH:], group_pairs)
    cross_mask = cross_allowed(token_counts, block_len)
    partial_mixed, cross_top, cross_total = cross_forward(
        group_queries, cross_keys, cross_values, cross_mask
    )
    partial_rows = partial_mixed.reshape(group_caps * SEQ, MODEL_WIDTH)
    cross_full = lax.psum(partial_rows, "img")
    own_start = lax.axis_index("img") * total_row_count
    own_full = lax.dynamic_slice_in_dim(cross_full, own_start, total_row_count, 0)
    cross_mixed = own_full.astype(jnp.bfloat16)
    second_sum = first_sum + matmul(cross_mixed, cout_w) + shift_rows[8]
    normed3 = layer_norm(second_sum, gain_rows[2], shift_rows[2]).astype(jnp.bfloat16)
    hidden = matmul(normed3, in_w) + inner_bias
    activated = jax.nn.gelu(hidden, approximate=False).astype(jnp.bfloat16)
    result = second_sum + matmul(activated, outm_w) + shift_rows[9]
    layer_out = result.reshape(tokens.shape).astype(jnp.bfloat16)
    grad_low3 = cotangent.reshape(total_row_count, MODEL_WIDTH)
    grad_result = grad_low3.astype(jnp.float32)
    g_outm = matmul_tleft(activated, grad_low3)
    g_shift9 = column_sums(grad_low3)
    grad_act = matmul_tright(grad_low3, outm_w)
    _, gelu_pull = jax.vjp(lambda pre_act: jax.nn.gelu(pre_act, approximate=False), hidden)
    grad_hidden = gelu_pull(grad_act)[0].astype(jnp.bfloat16)
    g_in = matmul_tleft(normed3, grad_hidden)
    g_inner_bias = column_sums(grad_hidden)
    grad_normed3 = matmul_tright(grad_hidden, in_w)
    _, norm_pull3 = jax.vjp(layer_norm, second_sum, gain_rows[2], shift_rows[2])
    grad_second_ln, g_gain2, g_shift2 = norm_pull3(grad_normed3)
    grad_second = grad_result + grad_second_ln
    grad_low2 = grad_second.astype(jnp.bfloat16)
    g_cout = matmul_tleft(cross_mixed, grad_low2)
    g_shift8 = column_sums(grad_low2)
    grad_cross_mixed = matmul_tright(grad_low2, cout_w).astype(jnp.bfloat16)
    group_grad_rows = lax.all_gather(grad_cross_mixed, "img", axis=0, tiled=True)
    group_grads = to_heads(group_grad_rows, group_pairs)
    partial_query, grad_ckeys, grad_cvalues = cross_backward(
        group_queries, cross_keys, cross_values, cross_mask, cross_top, cross_total, group_grads
    )
    grad_query = lax.psum_scatter(
        partial_query.reshape(group_caps * SEQ, MODEL_WIDTH), "img", scatter_dimension=0, tiled=True
    ).astype(jnp.bfloat16)
    g_cq = matmul_tleft(normed2, grad_query)
    g_shift6 = column_sums(grad_query)
    grad_normed2 = matmul_tright(grad_query, cq_w)
    grad_value_rows = grad_cvalues.reshape(group_caps * block_len, MODEL_WIDTH)
    grad_image_kv = jnp.concatenate(
        [grad_ckeys.reshape(group_caps * block_len, MODEL_WIDTH), grad_value_rows], axis=1
    )
    g_ckv = matmul_tleft(image_rows, grad_image_kv)
    g_shift7 = column_sums(grad_value_rows)
    image_grads = (
        matmul_tright(grad_image_kv, ckv_w).reshape(image_tokens.shape).astype(jnp.bfloat16)
    )
    _, norm_pull2 = jax.vjp(layer_norm, first_sum, gain_rows[1], shift_rows[1])
    grad_first_ln, g_gain1, g_shift1 = norm_pull2(grad_normed2)
    grad_first = grad_second + grad_first_ln
    grad_low1 = grad_first.astype(jnp.bfloat16)
    g_sout = matmul_tleft(self_mixed, grad_low1)
    g_shift5 = column_sums(grad_low1)
    grad_self_mixed = to_heads(matmul_tright(grad_low1, sout_w).astype(jnp.bfloat16), pair_count)
    self_query_gradient, self_key_gradient, self_value_gradient = self_attention_backward(
        self_queries, self_keys, self_values, causal, self_logs, grad_self_mixed
    )
    query_rows_gradient = self_query_gradient.reshape(total_row_count, MODEL_WIDTH).astype(
        jnp.bfloat16
    )
    value_self_gradient = self_value_gradient.reshape(total_row_count, MODEL_WIDTH)
    grad_qkv = jnp.concatenate(
        [
            query_rows_gradient,
            self_key_gradient.reshape(total_row_count, MODEL_WIDTH),
            value_self_gradient,
        ],
        axis=1,
    )
    g_qkv = matmul_tleft(normed1, grad_qkv)
    g_shift3 = column_sums(query_rows_gradient)
    g_shift4 = column_sums(value_self_gradient)
    grad_normed1 = matmul_tright(grad_qkv, qkv_w)
    _, norm_pull1 = jax.vjp(layer_norm, rows, gain_rows[0], shift_rows[0])
    grad_rows_ln, g_gain0, g_shift0 = norm_pull1(grad_normed1)
    token_grads = (grad_first + grad_rows_ln).reshape(tokens.shape).astype(jnp.bfloat16)
    g_gains = jnp.stack([g_gain0, g_gain1, g_gain2])
    g_shift_rows = jnp.stack(
        [
            g_shift0,
            g_shift1,
            g_shift2,
            g_shift3,
            g_shift4,
            g_shift5,
            g_shift6,
            g_shift7,
            g_shift8,
            g_shift9,
        ]
    )
    tall_grads = (
        lax.psum_scatter(g_qkv, "dp", scatter_dimension=0, tiled=True),
        lax.psum_scatter(g_sout, "dp", scatter_dimension=0, tiled=True),
        lax.psum_scatter(g_cq, "dp", scatter_dimension=0, tiled=True),
        lax.psum_scatter(g_ckv, "dp", scatter_dimension=0, tiled=True),
        lax.psum_scatter(g_cout, "dp", scatter_dimension=0, tiled=True),
        lax.psum_scatter(g_in, "dp", scatter_dimension=0, tiled=True),
        lax.psum_scatter(g_outm, "dp", scatter_dimension=0, tiled=True),
        lax.psum_scatter(g_gains, "dp", scatter_dimension=1, tiled=True),
        lax.psum_scatter(g_shift_rows, "dp", scatter_dimension=1, tiled=True),
        lax.psum_scatter(g_inner_bias, "dp", scatter_dimension=0, tiled=True),
    )
    mat_grads = (
        lax.psum_scatter(tall_grads[0], "img", scatter_dimension=1, tiled=True),
        lax.psum_scatter(tall_grads[1], "img", scatter_dimension=1, tiled=True),
        lax.psum_scatter(tall_grads[2], "img", scatter_dimension=1, tiled=True),
        lax.psum_scatter(tall_grads[3], "img", scatter_dimension=1, tiled=True),
        lax.psum_scatter(tall_grads[4], "img", scatter_dimension=1, tiled=True),
        lax.psum_scatter(tall_grads[5], "img", scatter_dimension=1, tiled=True),
        lax.psum_scatter(tall_grads[6], "img", scatter_dimension=1, tiled=True),
    )
    vector_sums = lax.psum((tall_grads[7], tall_grads[8], tall_grads[9]), "img")
    return (
        layer_out,
        token_grads,
        image_grads,
        mat_grads[0],
        mat_grads[1],
        mat_grads[2],
        mat_grads[3],
        mat_grads[4],
        mat_grads[5],
        mat_grads[6],
        vector_sums[0],
        vector_sums[1],
        vector_sums[2],
    )


def solution(mesh):
    in_specs = (
        P(("dp", "img"), None, None),
        P("dp", "img", None),
        P("dp"),
        P("dp", "img"),
        P("dp", "img"),
        P("dp", "img"),
        P("dp", "img"),
        P("dp", "img"),
        P("dp", "img"),
        P("dp", "img"),
        P(None, "dp"),
        P(None, "dp"),
        P("dp"),
        P(("dp", "img"), None, None),
    )
    out_specs = (
        P(("dp", "img"), None, None),
        P(("dp", "img"), None, None),
        P("dp", "img", None),
        P("dp", "img"),
        P("dp", "img"),
        P("dp", "img"),
        P("dp", "img"),
        P("dp", "img"),
        P("dp", "img"),
        P("dp", "img"),
        P(None, "dp"),
        P(None, "dp"),
        P("dp"),
    )
    return jax.shard_map(local, mesh=mesh, in_specs=in_specs, out_specs=out_specs, check_vma=False)
```

profile of v0, /device:TPU:0, one launch (start us, length us, event | category | flops | bytes accessed | tf_op | source)
XLA Modules:
  0.0 1494.6 jit_solution(12224464990832201736)
XLA Ops:
  7.3 17.3 %all-gather.4 = bf16[4,576,96]{1,2,0:T(8,128)(2,1)S(1)} all-gather(bf16[1,576,96]{1,2,0:T(8,128)(2,1)} %bitcast.271), channel_id=1, replica_groups=mesh['dp'=8,'img'=4] {'img'}, dimensions={0}, use_global_device_ids=true | all-gather | bytes 552960 | tf_op jit(solution)/shard_map/all_gather | solution.py:176
  58.7 15.0 %all_gather.75 = bf16[96,1536]{1,0:T(8,128)(2,1)} all-gather(bf16[96,384]{1,0:T(8,128)(2,1)S(1)} %copy-done.42), channel_id=1, replica_groups=mesh['dp'=8,'img'=4] {'img'}, dimensions={1}, use_global_device_ids=true | all-gather | bytes 368640 | tf_op jit(solution)/shard_map/all_gather | solution.py:179
  148.5 20.6 %all_gather.86 = bf16[96,3072]{1,0:T(8,128)(2,1)} all-gather(bf16[96,768]{1,0:T(8,128)(2,1)S(1)} %copy-done.37), channel_id=1, replica_groups=mesh['dp'=8,'img'=4] {'img'}, dimensions={1}, use_global_device_ids=true | all-gather | bytes 737280 | tf_op jit(solution)/shard_map/all_gather | solution.py:181
  169.1 23.7 %all_gather.89 = bf16[384,768]{0,1:T(8,128)(2,1)} all-gather(bf16[384,192]{0,1:T(8,128)(2,1)} %param.25), channel_id=1, replica_groups=mesh['dp'=8,'img'=4] {'img'}, dimensions={1}, use_global_device_ids=true | all-gather | bytes 737280 | tf_op jit(solution)/shard_map/all_gather | solution.py:182
  266.2 15.5 %all-gather = f32[64,12,128]{2,0,1:T(8,128)S(1)} all-gather(f32[16,12,128]{2,0,1:T(8,128)S(1)} %copy.228), channel_id=2, replica_groups=mesh['dp'=8,'img'=4] {'img'}, dimensions={0}, use_global_device_ids=true | all-gather | bytes 491520 | tf_op jit(solution)/shard_map/all_gather | solution.py:17
  303.3 209.1 %all-reduce.7 = bf16[2048,768]{0,1:T(8,128)(2,1)} all-reduce(f32[2048,768]{0,1:T(8,128)} %bitcast.234), channel_id=1, replica_groups=mesh['dp'=8,'img'=4] {'img'}, use_global_device_ids=true, to_apply=%region_10.11 | all-reduce | flops 1572864 | bytes 9437184 | tf_op jit(solution)/shard_map/psum | solution.py:234
  525.0 20.7 %convert_reduce_fusion = (f32[3072]{0:T(1024)}, bf16[512,3072]{1,0:T(8,128)(2,1)S(1)}, f32[512,3072]{1,0:T(8,128)}) fusion(f32[512,3072]{1,0:T(8,128)} %fusion.100, f32[3072]{0:T(1024)S(1)} %bitcast.275, bf16[512,768]{1,0:T(8,128)(2,1)} %bitcast.246, bf16[3072,768]{0,1:T(8,128)(2,1)} %all-gather.30.cloned.1.call-done), kind=kOutput, calls=%fused_computation.20 | convolution fusion | flops 2533880832 | bytes 21258240 | tf_op jit(solution)/shard_map/dot_general | solution.py:44
  553.5 64.5 %all-gather.32.cloned.1.call-done = bf16[2048,768]{1,0:T(8,128)(2,1)} async-done(((bf16[512,768]{1,0:T(8,128)(2,1)}), bf16[2048,768]{1,0:T(8,128)(2,1)}) %all-gather.32.cloned.1.call-update) | async-done | bytes 3145744 | tf_op jit(solution)/shard_map/all_gather | solution.py:261
  639.2 32.8 %all-reduce.6.cloned.1.call-done = f32[16,12,128]{2,1,0:T(8,128)} async-done(((f32[16,12,128]{2,1,0:T(8,128)}), f32[16,12,128]{2,1,0:T(8,128)}) %all-reduce.6.cloned.1.call-update) | async-done | bytes 98320 | tf_op jit(solution)/shard_map/psum | solution.py:154
  740.8 65.4 %reduce-scatter.34.cloned.1.call-done = f32[512,768]{0,1:T(8,128)} async-done(((f32[2048,768]{0,1:T(8,128)}), f32[512,768]{0,1:T(8,128)}) %reduce-scatter.34.cloned.1.call-update) | async-done | bytes 1572880 | tf_op jit(solution)/shard_map/reduce_scatter | solution.py:266
  871.5 38.6 %reduce-scatter.58.cloned.1.call-done = f32[96,1536]{1,0:T(8,128)} async-done(((f32[768,1536]{1,0:T(8,128)}), f32[96,1536]{1,0:T(8,128)}) %reduce-scatter.58.cloned.1.call-update) | async-done | bytes 589840
  923.0 33.2 %reduce-scatter.40.cloned.1.call-done = f32[96,768]{1,0:T(8,128)} async-done(((f32[768,768]{1,0:T(8,128)}), f32[96,768]{1,0:T(8,128)}) %reduce-scatter.40.cloned.1.call-update) | async-done | bytes 294928 | tf_op jit(solution)/shard_map/reduce_scatter | solution.py:328
  958.1 43.7 %reduce-scatter.38.cloned.1.call-done = f32[96,768]{1,0:T(8,128)} async-done(((f32[768,768]{1,0:T(8,128)}), f32[96,768]{1,0:T(8,128)}) %reduce-scatter.38.cloned.1.call-update) | async-done | bytes 294928 | tf_op jit(solution)/shard_map/reduce_scatter | solution.py:327
  1003.8 67.4 %reduce-scatter.36.cloned.1.call-done = f32[96,2304]{1,0:T(8,128)} async-done(((f32[768,2304]{1,0:T(8,128)}), f32[96,2304]{1,0:T(8,128)}) %reduce-scatter.36.cloned.1.call-update) | async-done | bytes 884752 | tf_op jit(solution)/shard_map/reduce_scatter | solution.py:326
  1073.8 77.2 %reduce-scatter.46.cloned.1.call-done = f32[96,3072]{1,0:T(8,128)} async-done(((f32[768,3072]{1,0:T(8,128)}), f32[96,3072]{1,0:T(8,128)}) %reduce-scatter.46.cloned.1.call-update) | async-done | bytes 1179664 | tf_op jit(solution)/shard_map/reduce_scatter | solution.py:331
  1152.4 23.4 %all-reduce.1 = f32[3072]{0:T(1024)S(1)} all-reduce(f32[3072]{0:T(1024)S(1)} %copy-done.64), channel_id=21, replica_groups=mesh['dp'=8,'img'=4] {'dp'}, use_global_device_ids=true, to_apply=%region_55.56.clone | all-reduce | flops 3072 | bytes 24576
  1175.9 55.0 %reduce-scatter.50.cloned.1.call-done = f32[384,768]{1,0:T(8,128)} async-done(((f32[3072,768]{1,0:T(8,128)}), f32[384,768]{1,0:T(8,128)}) %reduce-scatter.50.cloned.1.call-update) | async-done | bytes 1179664 | tf_op jit(solution)/shard_map/reduce_scatter | solution.py:332
  1283.6 31.1 %reduce-scatter.64.cloned.1.call-done = f32[96,3]{1,0:T(8,128)} async-done(((f32[768,3]{1,0:T(8,128)}), f32[96,3]{1,0:T(8,128)}) %reduce-scatter.64.cloned.1.call-update) | async-done | bytes 1168
  1315.6 36.3 %reduce-scatter.66.cloned.1.call-done = f32[96,10]{1,0:T(8,128)} async-done(((f32[768,10]{1,0:T(8,128)}), f32[96,10]{1,0:T(8,128)}) %reduce-scatter.66.cloned.1.call-update) | async-done | bytes 3856
  1352.8 19.3 %all-reduce.2 = (f32[3,96]{1,0:T(4,128)}, f32[10,96]{1,0:T(8,128)}, f32[384]{0:T(512)}) all-reduce(f32[3,96]{1,0:T(4,128)S(1)} %copy.286, f32[10,96]{1,0:T(8,128)S(1)} %copy.288, f32[384]{0:T(512)S(1)} %dynamic-slice.1), channel_id=1, replica_groups=mesh['dp'=8,'img'=4] {'img'}, use_global_device_ids=true, to_apply=%region_41.42 | all-reduce | flops 1632 | bytes 13056 | tf_op jit(solution)/shard_map/psum | solution.py:346
  1376.6 19.4 %reduce-scatter.54.cloned.1.call-done = f32[192,96]{1,0:T(8,128)} async-done(((f32[768,96]{1,0:T(8,128)}), f32[192,96]{1,0:T(8,128)}) %reduce-scatter.54.cloned.1.call-update) | async-done | bytes 73744
  1397.7 28.3 %reduce-scatter.52.cloned.1.call-done = f32[576,96]{1,0:T(8,128)} async-done(((f32[2304,96]{1,0:T(8,128)}), f32[576,96]{1,0:T(8,128)}) %reduce-scatter.52.cloned.1.call-update) | async-done | bytes 221200
  1427.8 29.0 %reduce-scatter.48.cloned.1.call-done = f32[96,768]{1,0:T(8,128)} async-done(((f32[96,3072]{1,0:T(8,128)}), f32[96,768]{1,0:T(8,128)}) %reduce-scatter.48.cloned.1.call-update) | async-done | bytes 294928 | tf_op jit(solution)/shard_map/reduce_scatter | solution.py:343
  1456.8 30.8 %reduce-scatter.62.cloned.1.call-done = f32[192,384]{1,0:T(8,128)} async-done(((f32[768,384]{1,0:T(8,128)}), f32[192,384]{1,0:T(8,128)}) %reduce-scatter.62.cloned.1.call-update) | async-done | bytes 294928
  (398 shorter events, 463.8 us)
Async XLA Ops:
  58.6 145.1 %all-gather.20.cloned.1.call-start = ((), (), s32[]{:S(2)}) async-start(), calls=%async_computation.19 | async-start | bytes 2654208 | tf_op jit(solution)/shard_map/all_gather | solution.py:188
  73.7 158.7 %all-gather.24.cloned.1.call-start = ((), (), s32[]{:S(2)}) async-start(), calls=%async_computation.21 | async-start | bytes 3932160 | tf_op jit(solution)/shard_map/all_gather | solution.py:222
  133.7 378.7 %all-gather.26.cloned.1.call-start = ((), (), s32[]{:S(2)}) async-start(), calls=%async_computation.22 | async-start | bytes 1327104 | tf_op jit(solution)/shard_map/all_gather | solution.py:189
  148.4 368.4 %all-gather.28.cloned.1.call-start = ((), (), s32[]{:S(2)}) async-start(), calls=%async_computation.23 | async-start | bytes 5308416 | tf_op jit(solution)/shard_map/all_gather | solution.py:190
  169.1 355.9 %all-gather.30.cloned.1.call-start = ((), (), s32[]{:S(2)}) async-start(), calls=%async_computation.24 | async-start | bytes 5308416 | tf_op jit(solution)/shard_map/all_gather | solution.py:191
  192.9 425.1 %all-gather.32.cloned.1.call-start = ((), (), s32[]{:S(2)}) async-start(), calls=%async_computation.25 | async-start | bytes 3932160 | tf_op jit(solution)/shard_map/all_gather | solution.py:261
  553.5 118.6 %all-reduce.6.cloned.1.call-start = ((), (), s32[]{:S(2)}) async-start(), calls=%async_computation.26 | async-start | bytes 262144 | tf_op jit(solution)/shard_map/psum | solution.py:154
  638.8 167.4 %reduce-scatter.34.cloned.1.call-start = ((), (), s32[]{:S(2)}) async-start(), calls=%async_computation.27 | async-start | bytes 7864320 | tf_op jit(solution)/shard_map/reduce_scatter | solution.py:266
  695.7 172.4 %reduce-scatter.44.cloned.1.call-start = ((), (), s32[]{:S(2)}) async-start(), calls=%async_computation.32 | async-start | bytes 2654208 | tf_op jit(solution)/shard_map/reduce_scatter | solution.py:330
  699.3 210.8 %reduce-scatter.58.cloned.1.call-start = ((), (), s32[]{:S(2)}) async-start(), calls=%async_computation.39 | async-start | bytes 5308416
  740.7 215.5 %reduce-scatter.40.cloned.1.call-start = ((), (), s32[]{:S(2)}) async-start(), calls=%async_computation.30 | async-start | bytes 2654208 | tf_op jit(solution)/shard_map/reduce_scatter | solution.py:328
  810.7 191.2 %reduce-scatter.38.cloned.1.call-start = ((), (), s32[]{:S(2)}) async-start(), calls=%async_computation.29 | async-start | bytes 2654208 | tf_op jit(solution)/shard_map/reduce_scatter | solution.py:327
  819.9 251.3 %reduce-scatter.36.cloned.1.call-start = ((), (), s32[]{:S(2)}) async-start(), calls=%async_computation.28 | async-start | bytes 7962624 | tf_op jit(solution)/shard_map/reduce_scatter | solution.py:326
  844.8 306.3 %reduce-scatter.46.cloned.1.call-start = ((), (), s32[]{:S(2)}) async-start(), calls=%async_computation.33 | async-start | bytes 10616832 | tf_op jit(solution)/shard_map/reduce_scatter | solution.py:331
  854.5 376.4 %reduce-scatter.50.cloned.1.call-start = ((), (), s32[]{:S(2)}) async-start(), calls=%async_computation.35 | async-start | bytes 10616832 | tf_op jit(solution)/shard_map/reduce_scatter | solution.py:332
  868.0 385.8 %reduce-scatter.60.cloned.1.call-start = ((), (), s32[]{:S(2)}) async-start(), calls=%async_computation.40 | async-start | bytes 491520
  870.0 408.3 %reduce-scatter.42.cloned.1.call-start = ((), (), s32[]{:S(2)}) async-start(), calls=%async_computation.31 | async-start | bytes 983040 | tf_op jit(solution)/shard_map/reduce_scatter | solution.py:341
  912.4 402.4 %reduce-scatter.64.cloned.1.call-start = ((), (), s32[]{:S(2)}) async-start(), calls=%async_computation.42 | async-start | bytes 442368
  919.9 432.1 %reduce-scatter.66.cloned.1.call-start = ((), (), s32[]{:S(2)}) async-start(), calls=%async_computation.43 | async-start | bytes 442368
  922.9 452.1 %reduce-scatter.56.cloned.1.call-start = ((), (), s32[]{:S(2)}) async-start(), calls=%async_computation.38 | async-start | bytes 491520
  958.1 438.0 %reduce-scatter.54.cloned.1.call-start = ((), (), s32[]{:S(2)}) async-start(), calls=%async_computation.37 | async-start | bytes 491520
  1003.8 422.2 %reduce-scatter.52.cloned.1.call-start = ((), (), s32[]{:S(2)}) async-start(), calls=%async_computation.36 | async-start | bytes 1474560
  1073.8 383.0 %reduce-scatter.48.cloned.1.call-start = ((), (), s32[]{:S(2)}) async-start(), calls=%async_computation.34 | async-start | bytes 1474560 | tf_op jit(solution)/shard_map/reduce_scatter | solution.py:343
  1151.1 336.5 %reduce-scatter.62.cloned.1.call-start = ((), (), s32[]{:S(2)}) async-start(), calls=%async_computation.41 | async-start | bytes 1474560
  (78 other events, 2205.5 us)
Sparse Core Ops, SparseCore 0:
  28.0 35.7 all-gather.15
  66.2 24.0 all-gather.17
  92.7 24.0 all-gather.21
  118.6 28.9 all-gather.19
  149.0 75.0 all-gather.23
  226.4 22.7 all-gather.25
  251.1 38.9 all-gather.27
  291.9 39.7 all-gather.29
  553.6 64.3 all-gather.31
  638.9 33.0 all-reduce.5
  695.8 110.3 reduce-scatter.33
  809.8 42.9 reduce-scatter.43
  856.2 53.8 reduce-scatter.57
  913.7 42.4 reduce-scatter.39
  959.4 42.4 reduce-scatter.37
  1005.7 65.4 reduce-scatter.35
  1074.5 76.4 reduce-scatter.45
  1154.4 76.4 reduce-scatter.49
  1256.6 21.6 reduce-scatter.41
  1281.7 32.9 reduce-scatter.63
  1318.1 33.8 reduce-scatter.65
  1398.5 27.4 reduce-scatter.51
  1428.8 27.8 reduce-scatter.47
  1459.6 27.8 reduce-scatter.61
  (3 shorter events, 59.9 us)
where the time goes:
time: 1500 us; the launch traced here: 1490 us
  waiting for transfers between devices  683 us (46%)
  blocking collectives  427 us (28%)
  matrix products  175 us (12%)
  local copies, waits for them, and re-layouts  152 us (10%)
  other arithmetic  39.1 us (3%)
  between operations  16.6 us (1%)
    psum x1, blocking collectives, local(): cross_full = lax.psum(partial_rows, 'img')  209 us
    unnamed x35, waiting for transfers between devices  201 us
    unnamed x182, local copies, waits for them, and re-layouts  82.1 us
    reduce_scatter x1, waiting for transfers between devices, local(): lax.psum_scatter(g_in, 'dp', scatter_dimension=0, tiled=True)  77.2 us
    reduce_scatter x1, waiting for transfers between devices, local(): lax.psum_scatter(g_qkv, 'dp', scatter_dimension=0, tiled=True)  67.4 us
    reduce_scatter x1, waiting for transfers between devices, local(): lax.psum_scatter(partial_query.reshape(group_caps * SEQ, MODEL_WIDTH), 'i...  65.4 us
    all_gather x1, waiting for transfers between devices, local(): lax.all_gather(grad_cross_mixed, 'img', axis=0, tiled=True)  64.5 us
    reduce_scatter x1, waiting for transfers between devices, local(): lax.psum_scatter(g_outm, 'dp', scatter_dimension=0, tiled=True)  55 us
  transfers between devices with their start and end apart: 27, of which 18 were waited for; matrix products, arithmetic and copies ran while one was open for 18% of the time, Pallas kernels for 0%

commit v1 on v0

v1 whole, which is shorter than its diff:
```python
import functools

import jax
import jax.numpy as jnp
from jax import lax
from jax.experimental import pallas as pl
from jax.experimental.pallas import tpu as pltpu
from jax.sharding import PartitionSpec as P

MODEL_WIDTH = 768
HEADS = 12
HEAD = 64
SEQ = 64
VEC_ROWS = 16
LANES = 128
MESH = pl.DeviceIdType.MESH
bf16 = jnp.bfloat16
f32 = jnp.float32

masked_value = -1e30
norm_epsilon = 1e-05


def tile_ds(index, size, unit):
    return pl.ds(pl.multiple_of(index * size, unit), size)


def stacked_block(rows, cols):
    return lambda ref, d, i: ref.at[i, tile_ds(d, rows, 16), :]


def grid_block(rows, cols):
    return lambda ref, d, i: ref.at[tile_ds(d, rows, 16), tile_ds(i, cols, LANES)]


def turned_block(rows, cols):
    return lambda ref, d, i: ref.at[tile_ds(i, rows, 16), tile_ds(d, cols, LANES)]


class Group:
    def __init__(self, rows, cols, dtype, full, block):
        self.rows, self.cols, self.dtype, self.full = rows, cols, dtype, full
        self.block = block(rows, cols)


def flip(d, bit):
    return d + bit * (1 - 2 * ((d // bit) % 2))


class Place:
    def __init__(self, n_img):
        self.n_img = n_img
        self.dp, self.im = lax.axis_index("dp"), lax.axis_index("img")
        self.core = self.dp % 2
        self.sib = flip(self.dp, 1)

    def first(self, d):
        return flip(d, 2) * (1 - self.core) + flip(d, 4) * self.core

    def second(self, d):
        return flip(d, 4) * (1 - self.core) + flip(d, 2) * self.core

    def near(self, k):
        value = jnp.int32(0)
        for at in range(self.n_img):
            order = sorted(range(self.n_img), key=lambda other: (abs(other - at), other))
            value = jnp.where(self.im == at, order[k], value)
        return value

    def barrier(self):
        semaphore = pltpu.get_barrier_semaphore()
        peers = [(self.sib, self.im), (self.first(self.dp), self.im), (self.second(self.dp), self.im)]
        peers += [(self.dp, (self.im + k) % self.n_img) for k in range(1, self.n_img)]
        for peer in peers:
            pl.semaphore_signal(semaphore, inc=1, device_id=peer, device_id_type=MESH)
        pl.semaphore_wait(semaphore, len(peers))


class Sends:
    def __init__(self):
        self.started = []

    def send(self, src, dst, send_sem, recv_sem, device, when=None):
        copy = pltpu.make_async_remote_copy(
            src, dst, send_sem, recv_sem, device_id=device, device_id_type=MESH
        )
        self.started.append((when, copy))
        if when is None:
            copy.start()
        else:
            pl.when(when)(copy.start)

    def finish(self):
        for when, copy in self.started:
            if when is None:
                copy.wait_send()
            else:
                pl.when(when)(copy.wait_send)


def gather_kernel(groups, n_img, caps, *refs):
    count = len(groups)
    own, x_ref = refs[:count], refs[count]
    full, xo_ref = refs[count + 1 : 2 * count + 1], refs[2 * count + 1]
    send_sem, recv_sem, local_sem, xs_sem, xr_sem = refs[2 * count + 2 :]
    here = Place(n_img)
    dp, im, sib = here.dp, here.im, here.sib
    near = [here.near(k) for k in range(n_img)]
    sends = Sends()
    used = [0] * count

    locals_ = []
    for g, group in enumerate(groups):
        copy = pltpu.make_async_copy(own[g], group.block(full[g], dp, im), local_sem.at[g])
        copy.start()
        locals_.append(copy)
    copy = pltpu.make_async_copy(
        x_ref.at[pl.ds(im * caps, caps)], xo_ref.at[im], local_sem.at[count]
    )
    copy.start()
    locals_.append(copy)
    here.barrier()

    def forward(g, d, i, src, device, when=None):
        sends.send(
            src,
            groups[g].block(full[g], d, i),
            send_sem.at[g, used[g]],
            recv_sem.at[g, d, i],
            device,
            when,
        )
        used[g] += 1

    def arrived(g, d, i):
        block = groups[g].block(full[g], d, i)
        pltpu.make_async_remote_copy(
            block, block, send_sem.at[g, 0], recv_sem.at[g, d, i], device_id=(sib, im), device_id_type=MESH
        ).wait_recv()
        return block

    for g in range(count):
        forward(g, dp, im, own[g], (dp, im + 1), im < n_img - 1)
        forward(g, dp, im, own[g], (dp, im - 1), im > 0)
        forward(g, dp, im, own[g], (here.first(dp), im))
        forward(g, dp, im, own[g], (here.second(dp), im))
        forward(g, dp, im, own[g], (sib, im))
    x_copies = []
    for k in range(1, n_img):
        target = (im + k) % n_img
        x_copies.append(
            pltpu.make_async_remote_copy(
                x_ref.at[pl.ds(target * caps, caps)],
                xo_ref.at[im],
                xs_sem.at[k],
                xr_sem.at[k],
                device_id=(dp, target),
                device_id_type=MESH,
            )
        )
        x_copies[-1].start()

    def line_step(g, k):
        i = near[k]
        block = arrived(g, dp, i)
        step = jnp.where(i < im, 1, -1)
        forward(g, dp, i, block, (dp, im + step), (im + step >= 0) & (im + step < n_img))
        forward(g, dp, i, block, (here.first(dp), im))
        forward(g, dp, i, block, (here.second(dp), im))
        forward(g, dp, i, block, (sib, im))

    def first_step(g, k):
        d, i = here.first(dp), near[k]
        block = arrived(g, d, i)
        forward(g, d, i, block, (here.second(dp), im))
        forward(g, d, i, block, (sib, im))

    def second_step(g, k):
        for d in (here.second(dp), here.second(here.first(dp))):
            block = arrived(g, d, near[k])
            forward(g, d, near[k], block, (sib, im))

    for t in range(count + 2):
        if t < count:
            for k in range(1, n_img):
                line_step(t, k)
        if 0 <= t - 1 < count:
            for k in range(n_img):
                first_step(t - 1, k)
        if 0 <= t - 2 < count:
            for k in range(n_img):
                second_step(t - 2, k)
    for g in range(count):
        for c in range(4):
            for i in range(n_img):
                arrived(g, 2 * c + 1 - here.core, i)
    for copy in x_copies:
        copy.wait()
    sends.finish()
    for copy in locals_:
        copy.wait()


def gather_all(groups, n_img, owns, image_tokens):
    caps = image_tokens.shape[0] // n_img
    count = len(groups)
    any_spec = pl.BlockSpec(memory_space=pl.ANY)
    outs = [jax.ShapeDtypeStruct(group.full, group.dtype) for group in groups]
    outs.append(jax.ShapeDtypeStruct((n_img, caps) + image_tokens.shape[1:], image_tokens.dtype))
    dma = pltpu.SemaphoreType.DMA
    return pl.pallas_call(
        functools.partial(gather_kernel, groups, n_img, caps),
        out_shape=outs,
        in_specs=[any_spec] * (count + 1),
        out_specs=[any_spec] * (count + 1),
        scratch_shapes=[
            dma((count, 64)),
            dma((count, 8, n_img)),
            dma((count + 1,)),
            dma((n_img,)),
            dma((n_img,)),
        ],
        compiler_params=pltpu.CompilerParams(
            collective_id=1, has_side_effects=True, vmem_limit_bytes=8 << 20
        ),
    )(*owns, image_tokens)


def add_into(dst, src):
    rows = dst.shape[0]

    def body(r, carry):
        part = pl.ds(pl.multiple_of(r * 16, 16), 16)
        dst[part, :] = (dst[part, :].astype(f32) + src[part, :].astype(f32)).astype(dst.dtype)
        return carry

    lax.fori_loop(0, rows // 16, body, 0)


def reduce_kernel(groups, n_img, caps, *refs):
    count = len(groups)
    full, dx_ref = refs[:count], refs[count]
    refs = refs[count + 1 :]
    out, dxo_ref = refs[:count], refs[count]
    refs = refs[count + 1 :]
    acc, r0, r1, r2, zr = [refs[n * count : (n + 1) * count] for n in range(5)]
    (load_sem, s0_sem, r0_sem, s1_sem, r1_sem, s2_sem, r2_sem, sz_sem, rz_sem, xs_sem, xr_sem, x_sem) = refs[
        5 * count :
    ]
    here = Place(n_img)
    dp, im, sib, core = here.dp, here.im, here.sib, here.core
    chip = dp // 2
    first, second = here.first(dp), here.second(dp)
    chip1, chip2 = first // 2, second // 2
    chip12 = here.second(first) // 2
    near = [here.near(k) for k in range(n_img)]
    sends = Sends()

    loads = {}
    for g, group in enumerate(groups):
        for c in range(4):
            for i in range(n_img):
                copy = pltpu.make_async_copy(
                    group.block(full[g], 2 * c + core, i), acc[g].at[c, i], load_sem.at[g, c, i]
                )
                copy.start()
    x_own = pltpu.make_async_copy(dx_ref.at[im], dxo_ref.at[pl.ds(im * caps, caps)], x_sem)
    x_own.start()
    here.barrier()
    for g, group in enumerate(groups):
        for c in (chip1, chip12, chip2, chip):
            for i in range(n_img):
                sends.send(
                    group.block(full[g], 2 * c + 1 - core, i),
                    r0[g].at[c, i],
                    s0_sem.at[g, c, i],
                    r0_sem.at[g, c, i],
                    (sib, im),
                )
    x_copies = []
    for k in range(1, n_img):
        target = (im + k) % n_img
        copy = pltpu.make_async_remote_copy(
            dx_ref.at[target],
            dxo_ref.at[pl.ds(im * caps, caps)],
            xs_sem.at[k],
            xr_sem.at[k],
            device_id=(dp, target),
            device_id_type=MESH,
        )
        copy.start()
        x_copies.append(copy)

    def arrived(buffer, semaphore):
        pltpu.make_async_remote_copy(
            buffer, buffer, s0_sem.at[0, 0, 0], semaphore, device_id=(sib, im), device_id_type=MESH
        ).wait_recv()

    def own_pair(g, c, i):
        block = acc[g].at[c, i]
        pltpu.make_async_copy(block, block, load_sem.at[g, c, i]).wait()
        arrived(r0[g].at[c, i], r0_sem.at[g, c, i])
        add_into(block, r0[g].at[c, i])
        return block

    def take(block, buffer, semaphore):
        arrived(buffer, semaphore)
        add_into(block, buffer)

    def second_step(g):
        for j, c in enumerate((chip2, chip12)):
            for i in range(n_img):
                block = own_pair(g, c, i)
                sends.send(
                    block, r1[g].at[j, i], s1_sem.at[g, j, i], r1_sem.at[g, j, i], (second, im)
                )

    def first_step(g):
        for i in range(n_img):
            block = own_pair(g, chip1, i)
            take(block, r1[g].at[1, i], r1_sem.at[g, 1, i])
            sends.send(block, r2[g].at[i], s2_sem.at[g, i], r2_sem.at[g, i], (first, im))

    def line_step(g):
        for k in reversed(range(1, n_img)):
            i = near[k]
            block = own_pair(g, chip, i)
            take(block, r1[g].at[0, i], r1_sem.at[g, 0, i])
            take(block, r2[g].at[i], r2_sem.at[g, i])
            down = jnp.where(i < im, 1, 0)
            inner = (im > 0) & (im < n_img - 1)

            @pl.when(inner)
            def _():
                take(block, zr[g].at[down, i], rz_sem.at[g, down, i])

            sends.send(
                block,
                zr[g].at[down, i],
                sz_sem.at[g, i],
                rz_sem.at[g, down, i],
                (dp, im + 1 - 2 * down),
            )
        block = own_pair(g, chip, im)
        take(block, r1[g].at[0, im], r1_sem.at[g, 0, im])
        take(block, r2[g].at[im], r2_sem.at[g, im])

    def last_step(g):
        block = acc[g].at[chip, im]
        out[g][...] = block[...].astype(f32)
        for down, has in ((0, im > 0), (1, im < n_img - 1)):

            @pl.when(has)
            def _():
                arrived(zr[g].at[down, im], rz_sem.at[g, down, im])
                out[g][...] += zr[g][down, im].astype(f32)

    for t in range(count + 3):
        if t < count:
            second_step(t)
        if 0 <= t - 1 < count:
            first_step(t - 1)
        if 0 <= t - 2 < count:
            line_step(t - 2)
        if 0 <= t - 3 < count:
            last_step(t - 3)
    for copy in x_copies:
        copy.wait()
    sends.finish()
    x_own.wait()


def reduce_all(groups, n_img, partials, image_grads):
    caps = image_grads.shape[1]
    count = len(groups)
    any_spec = pl.BlockSpec(memory_space=pl.ANY)
    vmem_spec = pl.BlockSpec(memory_space=pltpu.VMEM)
    outs = [jax.ShapeDtypeStruct((group.rows, group.cols), f32) for group in groups]
    outs.append(
        jax.ShapeDtypeStruct((n_img * caps,) + image_grads.shape[2:], image_grads.dtype)
    )
    dma = pltpu.SemaphoreType.DMA

    def buffers(*lead):
        return [pltpu.VMEM(lead + (group.rows, group.cols), group.dtype) for group in groups]

    return pl.pallas_call(
        functools.partial(reduce_kernel, groups, n_img, caps),
        out_shape=outs,
        in_specs=[any_spec] * (count + 1),
        out_specs=[vmem_spec] * count + [any_spec],
        scratch_shapes=buffers(4, n_img)
        + buffers(4, n_img)
        + buffers(2, n_img)
        + buffers(n_img)
        + buffers(2, n_img)
        + [
            dma((count, 4, n_img)),
            dma((count, 4, n_img)),
            dma((count, 4, n_img)),
            dma((count, 2, n_img)),
            dma((count, 2, n_img)),
            dma((count, n_img)),
            dma((count, n_img)),
            dma((count, n_img)),
            dma((count, 2, n_img)),
            dma((n_img,)),
            dma((n_img,)),
            dma(()),
        ],
        compiler_params=pltpu.CompilerParams(
            collective_id=2, has_side_effects=True, vmem_limit_bytes=56 << 20
        ),
    )(*partials, image_grads)


def layer_norm(values, norm_gain, norm_shift):
    average = jnp.mean(values, axis=-1, keepdims=True)
    centred = values - average
    spread = jnp.mean(centred * centred, axis=-1, keepdims=True)
    return centred * lax.rsqrt(spread + norm_epsilon) * norm_gain + norm_shift


def matmul(left_op, right_op):
    return jnp.dot(left_op, right_op, preferred_element_type=f32)


def matmul_tleft(left_op, right_op):
    return lax.dot_general(
        left_op, right_op, (((0,), (0,)), ((), ())), preferred_element_type=f32
    )


def matmul_tright(left_op, right_op):
    return lax.dot_general(
        left_op, right_op, (((1,), (1,)), ((), ())), preferred_element_type=f32
    )


def column_sums(values):
    return jnp.sum(values.astype(f32), axis=0)


def to_heads(values, captions):
    return values.reshape(captions, -1, HEADS, HEAD)


def probabilities(queries, key_heads, allowed):
    scores = jnp.einsum("cqhd,ckhd->chqk", queries, key_heads, preferred_element_type=f32)
    scores = jnp.where(allowed, scores * HEAD ** (-0.5), masked_value)
    return jax.nn.softmax(scores, axis=-1)


def attention(queries, key_heads, value_heads, allowed):
    probs = probabilities(queries, key_heads, allowed).astype(bf16)
    return jnp.einsum("chqk,ckhd->cqhd", probs, value_heads, preferred_element_type=f32)


def attention_backward(queries, key_heads, value_heads, allowed, grad_mixed):
    probs = probabilities(queries, key_heads, allowed)
    grad_probs = jnp.einsum("cqhd,ckhd->chqk", grad_mixed, value_heads, preferred_element_type=f32)
    inner_term = jnp.sum(probs * grad_probs, axis=-1, keepdims=True)
    grad_scores = (probs * (grad_probs - inner_term)).astype(bf16)
    score_scale = HEAD ** (-0.5)
    grad_queries = (
        jnp.einsum("chqk,ckhd->cqhd", grad_scores, key_heads, preferred_element_type=f32)
        * score_scale
    )
    grad_keys = (
        jnp.einsum("chqk,cqhd->ckhd", grad_scores, queries, preferred_element_type=f32)
        * score_scale
    )
    grad_values = jnp.einsum(
        "chqk,cqhd->ckhd", probs.astype(bf16), grad_mixed, preferred_element_type=f32
    )
    return grad_queries.astype(bf16), grad_keys.astype(bf16), grad_values.astype(bf16)


def local(
    n_dp,
    n_img,
    tokens,
    image_tokens,
    token_counts,
    self_qkv,
    self_out,
    cross_q,
    cross_kv,
    cross_out,
    mlp_in,
    mlp_out,
    norm_gains,
    shifts,
    mlp_bias,
    cotangent,
):
    captions = tokens.shape[0]
    rows_all = captions * SEQ
    block_len = image_tokens.shape[1]
    width = self_out.shape[1]
    depth = self_out.shape[0]
    inner_dp = mlp_out.shape[0]
    inner_img = mlp_in.shape[1]
    inner = inner_dp * n_dp
    direct = n_dp == 8 and depth % 16 == 0 and width % 16 == 0
    counts = lax.dynamic_slice_in_dim(token_counts, lax.axis_index("img") * captions, captions)

    mixed = jnp.concatenate([self_qkv, self_out, cross_q, cross_out], axis=1)
    vectors = jnp.concatenate([norm_gains.reshape(-1), shifts.reshape(-1), mlp_bias])
    if direct:
        used = vectors.shape[0]
        vectors = jnp.pad(vectors, (0, VEC_ROWS * LANES - used)).reshape(VEC_ROWS, LANES)
        groups = [
            Group(VEC_ROWS, LANES, f32, (n_img, n_dp * VEC_ROWS, LANES), stacked_block),
            Group(depth, 6 * width, bf16, (n_img, n_dp * depth, 6 * width), stacked_block),
            Group(depth, 2 * width, bf16, (MODEL_WIDTH, 2 * MODEL_WIDTH), grid_block),
            Group(depth, inner_img, bf16, (MODEL_WIDTH, inner), grid_block),
            Group(width, inner_dp, bf16, (MODEL_WIDTH, inner), turned_block),
        ]
        vec_full, mixed_full, ckv_w, in_w, outm_t, image_own = gather_all(
            groups, n_img, (vectors, mixed, cross_kv, mlp_in, mlp_out.T), image_tokens
        )
        vec_full = vec_full[0].reshape(n_dp, VEC_ROWS * LANES)[:, :used]
    else:

        def everything(block, first, then, axes):
            return lax.all_gather(
                lax.all_gather(block, first, axis=axes[0], tiled=True), then, axis=axes[1], tiled=True
            )

        mixed_full = lax.all_gather(
            lax.all_gather(mixed, "dp", axis=0, tiled=True), "img", axis=0, tiled=False
        )
        ckv_w = everything(cross_kv, "img", "dp", (1, 0))
        in_w = everything(mlp_in, "img", "dp", (1, 0))
        outm_t = everything(mlp_out, "img", "dp", (1, 0)).T
        vec_full = lax.all_gather(vectors, "dp", axis=0, tiled=False)
        image_own = lax.all_to_all(
            image_tokens.reshape((n_img, captions) + image_tokens.shape[1:]), "img", 0, 0, tiled=True
        )

    def columns(start, size):
        return (
            mixed_full[:, :, start * width : (start + size) * width]
            .transpose(1, 0, 2)
            .reshape(MODEL_WIDTH, size * MODEL_WIDTH)
        )

    qkv_w, sout_w, cq_w, cout_w = columns(0, 3), columns(3, 1), columns(4, 1), columns(5, 1)
    gain_rows = vec_full[:, : 3 * depth].reshape(n_dp, 3, depth).transpose(1, 0, 2).reshape(3, -1)
    shift_rows = (
        vec_full[:, 3 * depth : 13 * depth]
        .reshape(n_dp, 10, depth)
        .transpose(1, 0, 2)
        .reshape(10, -1)
    )
    inner_bias = vec_full[:, 13 * depth :].reshape(-1)

    zero_row = jnp.zeros((MODEL_WIDTH,), f32)
    rows = tokens.reshape(rows_all, MODEL_WIDTH).astype(f32)
    normed1 = layer_norm(rows, gain_rows[0], shift_rows[0]).astype(bf16)
    mixed_qkv = (
        matmul(normed1, qkv_w) + jnp.concatenate([shift_rows[3], zero_row, shift_rows[4]])
    ).astype(bf16)
    self_queries, self_keys, self_values = [
        to_heads(mixed_qkv[:, n * MODEL_WIDTH : (n + 1) * MODEL_WIDTH], captions) for n in range(3)
    ]
    places = jnp.arange(SEQ, dtype=jnp.int32)
    causal = (places[None, :] <= places[:, None])[None, None]
    self_mixed = attention(self_queries, self_keys, self_values, causal)
    self_mixed = self_mixed.reshape(rows_all, MODEL_WIDTH).astype(bf16)
    first_sum = rows + matmul(self_mixed, sout_w) + shift_rows[5]
    normed2 = layer_norm(first_sum, gain_rows[1], shift_rows[1]).astype(bf16)
    cross_query = (matmul(normed2, cq_w) + shift_rows[6]).astype(bf16)
    cross_queries = to_heads(cross_query, captions)

    image_len = n_img * block_len
    image_rows = image_own.reshape(n_img * captions * block_len, MODEL_WIDTH)
    image_kv = (matmul(image_rows, ckv_w) + jnp.concatenate([zero_row, shift_rows[7]])).astype(bf16)

    def by_caption(values):
        return (
            values.reshape(n_img, captions, block_len, HEADS, HEAD)
            .transpose(1, 0, 2, 3, 4)
            .reshape(captions, image_len, HEADS, HEAD)
        )

    def by_place(values):
        return (
            values.reshape(captions, n_img, block_len, MODEL_WIDTH)
            .transpose(1, 0, 2, 3)
            .reshape(-1, MODEL_WIDTH)
        )

    cross_keys = by_caption(image_kv[:, :MODEL_WIDTH])
    cross_values = by_caption(image_kv[:, MODEL_WIDTH:])
    valid = (jnp.arange(image_len, dtype=jnp.int32)[None, :] < counts[:, None])[:, None, None, :]
    cross_mixed = attention(cross_queries, cross_keys, cross_values, valid)
    cross_mixed = cross_mixed.reshape(rows_all, MODEL_WIDTH).astype(bf16)
    second_sum = first_sum + matmul(cross_mixed, cout_w) + shift_rows[8]
    normed3 = layer_norm(second_sum, gain_rows[2], shift_rows[2]).astype(bf16)
    hidden = matmul(normed3, in_w) + inner_bias
    activated = jax.nn.gelu(hidden, approximate=False).astype(bf16)
    result = second_sum + matmul_tright(activated, outm_t) + shift_rows[9]
    layer_out = result.reshape(tokens.shape).astype(bf16)

    grad_low3 = cotangent.reshape(rows_all, MODEL_WIDTH)
    g_outm_t = matmul_tleft(grad_low3, activated)
    g_shift9 = column_sums(grad_low3)
    grad_act = matmul(grad_low3, outm_t)
    _, gelu_pull = jax.vjp(lambda pre_act: jax.nn.gelu(pre_act, approximate=False), hidden)
    grad_hidden = gelu_pull(grad_act)[0].astype(bf16)
    g_in = matmul_tleft(normed3, grad_hidden)
    g_inner_bias = column_sums(grad_hidden)
    grad_normed3 = matmul_tright(grad_hidden, in_w)
    _, norm_pull3 = jax.vjp(layer_norm, second_sum, gain_rows[2], shift_rows[2])
    grad_second_ln, g_gain2, g_shift2 = norm_pull3(grad_normed3)
    grad_second = grad_low3.astype(f32) + grad_second_ln
    grad_low2 = grad_second.astype(bf16)
    g_cout = matmul_tleft(cross_mixed, grad_low2)
    g_shift8 = column_sums(grad_low2)
    grad_cross_mixed = to_heads(matmul_tright(grad_low2, cout_w).astype(bf16), captions)
    grad_query, grad_ckeys, grad_cvalues = attention_backward(
        cross_queries, cross_keys, cross_values, valid, grad_cross_mixed
    )
    grad_query = grad_query.reshape(rows_all, MODEL_WIDTH)
    g_cq = matmul_tleft(normed2, grad_query)
    g_shift6 = column_sums(grad_query)
    grad_normed2 = matmul_tright(grad_query, cq_w)
    grad_value_rows = by_place(grad_cvalues)
    grad_image_kv = jnp.concatenate([by_place(grad_ckeys), grad_value_rows], axis=1)
    g_ckv = matmul_tleft(image_rows, grad_image_kv)
    g_shift7 = column_sums(grad_value_rows)
    image_grads = matmul_tright(grad_image_kv, ckv_w).astype(bf16).reshape(image_own.shape)
    _, norm_pull2 = jax.vjp(layer_norm, first_sum, gain_rows[1], shift_rows[1])
    grad_first_ln, g_gain1, g_shift1 = norm_pull2(grad_normed2)
    grad_first = grad_second + grad_first_ln
    grad_low1 = grad_first.astype(bf16)
    g_sout = matmul_tleft(self_mixed, grad_low1)
    g_shift5 = column_sums(grad_low1)
    grad_self_mixed = to_heads(matmul_tright(grad_low1, sout_w).astype(bf16), captions)
    grad_qkv = jnp.concatenate(
        [
            part.reshape(rows_all, MODEL_WIDTH)
            for part in attention_backward(
                self_queries, self_keys, self_values, causal, grad_self_mixed
            )
        ],
        axis=1,
    )
    g_qkv = matmul_tleft(normed1, grad_qkv)
    qkv_sums = column_sums(grad_qkv)
    g_shift3, g_shift4 = qkv_sums[:MODEL_WIDTH], qkv_sums[2 * MODEL_WIDTH :]
    grad_normed1 = matmul_tright(grad_qkv, qkv_w)
    _, norm_pull1 = jax.vjp(layer_norm, rows, gain_rows[0], shift_rows[0])
    grad_rows_ln, g_gain0, g_shift0 = norm_pull1(grad_normed1)
    token_grads = (grad_first + grad_rows_ln).reshape(tokens.shape).astype(bf16)
    g_vector_rows = jnp.stack(
        [
            g_gain0,
            g_gain1,
            g_gain2,
            g_shift0,
            g_shift1,
            g_shift2,
            g_shift3,
            g_shift4,
            g_shift5,
            g_shift6,
            g_shift7,
            g_shift8,
            g_shift9,
        ]
    )

    if direct:
        g_vectors = jnp.concatenate(
            [
                g_vector_rows.reshape(13, n_dp, depth).transpose(1, 0, 2).reshape(n_dp, -1),
                g_inner_bias.reshape(n_dp, -1),
            ],
            axis=1,
        )
        g_vectors = jnp.pad(g_vectors, ((0, 0), (0, VEC_ROWS * LANES - used)))
        g_vectors = jnp.broadcast_to(
            g_vectors.reshape(1, n_dp * VEC_ROWS, LANES), (n_img, n_dp * VEC_ROWS, LANES)
        )

        def stacked(grad):
            return (
                grad.astype(bf16).reshape(MODEL_WIDTH, n_img, -1).transpose(1, 0, 2)
            )

        g_mixed = jnp.concatenate([stacked(g) for g in (g_qkv, g_sout, g_cq, g_cout)], axis=2)
        s_vectors, s_mixed, s_ckv, s_in, s_outm_t, image_out = reduce_all(
            groups,
            n_img,
            (g_vectors, g_mixed, g_ckv.astype(bf16), g_in.astype(bf16), g_outm_t.astype(bf16)),
            image_grads,
        )
        s_vectors = s_vectors.reshape(-1)
        s_rows = s_vectors[: 13 * depth].reshape(13, depth)
        s_inner = s_vectors[13 * depth : used]
        s_qkv = s_mixed[:, : 3 * width]
        s_sout, s_cq, s_cout = [s_mixed[:, n * width : (n + 1) * width] for n in (3, 4, 5)]
        s_outm = s_outm_t.T
    else:

        def scattered(grad):
            tall = lax.psum_scatter(grad, "dp", scatter_dimension=0, tiled=True)
            return lax.psum_scatter(tall, "img", scatter_dimension=1, tiled=True)

        s_qkv, s_sout, s_cq, s_ckv, s_cout, s_in, s_outm = [
            scattered(g) for g in (g_qkv, g_sout, g_cq, g_ckv, g_cout, g_in, g_outm_t.T)
        ]
        s_rows, s_inner = lax.psum(
            (
                lax.psum_scatter(g_vector_rows, "dp", scatter_dimension=1, tiled=True),
                lax.psum_scatter(g_inner_bias, "dp", scatter_dimension=0, tiled=True),
            ),
            "img",
        )
        image_out = lax.all_to_all(image_grads, "img", 0, 0, tiled=True).reshape(image_tokens.shape)
    return (
        layer_out,
        token_grads,
        image_out,
        s_qkv,
        s_sout,
        s_cq,
        s_ckv,
        s_cout,
        s_in,
        s_outm,
        s_rows[:3],
        s_rows[3:],
        s_inner,
    )


def solution(mesh):
    caption_rows = P(("dp", "img"), None, None)
    weight = P("dp", "img")
    vector = P(None, "dp")
    in_specs = (caption_rows, P("dp", "img", None), P("dp")) + (weight,) * 7
    in_specs += (vector, vector, P("dp"), caption_rows)
    out_specs = (caption_rows, caption_rows, P("dp", "img", None)) + (weight,) * 7
    out_specs += (vector, vector, P("dp"))
    return jax.shard_map(
        functools.partial(local, mesh.shape["dp"], mesh.shape["img"]),
        mesh=mesh,
        in_specs=in_specs,
        out_specs=out_specs,
        check_vma=False,
    )
```

time: 1500 us -> 740 us (0.49)
  waiting for transfers between devices: 683 us -> 0 us
  blocking collectives: 427 us -> 0 us
  Pallas kernels: 0 us -> 295 us
  local copies, waits for them, and re-layouts: 152 us -> 256 us
  matrix products: 175 us -> 144 us
    reduce_scatter x9 -> x0, waiting for transfers between devices: 385 us -> none  [the longest x1 77.2 us: local(): lax.psum_scatter(g_in, 'dp', scatter_dimension=0, tiled=True)]
    pallas_call x0 -> x2, Pallas kernels: none -> 295 us  [the longest x1 159 us: gather_all(): pl.pallas_call(functools.partial(gather_kernel, groups, n_img, caps), out...]
    psum x2 -> x0, blocking collectives: 228 us -> none  [the longest x1 209 us: local(): cross_full = lax.psum(partial_rows, 'img')]
    unnamed x35 -> x0, waiting for transfers between devices: 201 us -> none
    all_gather x12 -> x0, blocking collectives: 175 us -> none  [the longest x2 30.2 us: joined(): everything = jax.tree.map(lambda part: lax.all_gather(part, axis), value)]
    reshape x11 -> x32, local copies, waits for them, and re-layouts: 10.5 us -> 106 us  [the longest x11 34.3 us: to_heads(): return values.reshape(captions, -1, HEADS, HEAD)]
    all_gather x9 -> x0, waiting for transfers between devices: 64.5 us -> none  [the longest x1 64.5 us: local(): lax.all_gather(grad_cross_mixed, 'img', axis=0, tiled=True)]
    unnamed x182 -> x190, local copies, waits for them, and re-layouts: 82.1 us -> 25.5 us
  transfers between devices with their start and end apart: 27 -> 0, of which waited for: 18 -> 0; matrix products, arithmetic and copies ran while one was open for 18% -> 0% of each run, Pallas kernels for 0% -> 0%
where the time goes in v1:
time: 740 us; the launch traced here: 728 us
  Pallas kernels  295 us (40%)
  local copies, waits for them, and re-layouts  256 us (35%)
  matrix products  144 us (19%)
  other arithmetic  31.4 us (4%)
    pallas_call x1, Pallas kernels, gather_all(): pl.pallas_call(functools.partial(gather_kernel, groups, n_img, caps), out...  159 us
    pallas_call x1, Pallas kernels, reduce_all(): pl.pallas_call(functools.partial(reduce_kernel, groups, n_img, caps), out...  135 us
    dot_general x7, matrix products, matmul(): return jnp.dot(left_op, right_op, preferred_element_type=f32)  45.2 us
    reshape x11, local copies, waits for them, and re-layouts, to_heads(): return values.reshape(captions, -1, HEADS, HEAD)  34.3 us
    dot_general x7, matrix products, matmul_tleft(): lax.dot_general(left_op, right_op, (((0,), (0,)), ((), ())), preferred_el...  29.3 us
    dot_general x7, matrix products, matmul_tright(): lax.dot_general(left_op, right_op, (((1,), (1,)), ((), ())), preferred_el...  26.1 us
    unnamed x190, local copies, waits for them, and re-layouts  25.5 us
    reshape x2, local copies, waits for them, and re-layouts, by_caption(): values.reshape(n_img, captions, block_len, HEADS, HEAD)  20.6 us

profile of v1, /device:TPU:0, one launch (start us, length us, event | category | flops | bytes accessed | tf_op | source)
XLA Modules:
  0.0 727.7 jit_solution(8943563641232851054)
XLA Ops:
  12.1 159.2 %shard_map.237 = (f32[4,128,128]{2,1,0:T(8,128)S(1)}, bf16[4,768,1152]{2,1,0:T(8,128)(2,1)S(1)}, bf16[768,1536]{1,0:T(8,128)(2,1)S(1)}, bf16[768,3072]{1,0:T(8,1...) custom-call(f32[16,128]{1,0:T(8,128)S(1)} %pad_bitcast_fusion.refs_0_, ...), custom_call_target="tpu_custom_call" | custom-call | tf_op jit(solution)/shard_map/pallas_call | solution.py:211
  193.2 6.1 copy.48
  248.6 6.9 add_convert_fusion
  260.6 10.5 %reshape.411 = bf16[4,8,64,12,64]{2,1,0,4,3:T(8,128)(2,1)} reshape(bf16[2048,768]{0,1:T(8,128)(2,1)} %copy.62) | data formatting | bytes 6291456 | tf_op jit(solution)/shard_map/reshape | solution.py:583
  271.1 9.0 %copy.63 = bf16[8,4,64,12,64]{2,1,4,3,0:T(4,128)(2,1)} copy(bf16[8,4,64,12,64]{2,0,1,4,3:T(8,128)(2,1)} %bitcast.215) | data formatting | bytes 6291456 | tf_op jit(solution)/shard_map/transpose | solution.py:584
  280.1 8.7 %reshape.412 = bf16[8,256,12,64]{1,3,2,0:T(8,128)(2,1)S(1)} reshape(bf16[8,4,64,12,64]{2,1,4,3,0:T(4,128)(2,1)} %copy.63) | data formatting | bytes 6291456 | tf_op jit(solution)/shard_map/reshape | solution.py:585
  288.8 5.5 copy.58
  294.3 10.1 %reshape.407 = bf16[4,8,64,12,64]{2,1,0,4,3:T(8,128)(2,1)} reshape(bf16[2048,768]{0,1:T(8,128)(2,1)} %copy.58) | data formatting | bytes 6291456 | tf_op jit(solution)/shard_map/reshape | solution.py:583
  304.4 9.0 %copy.59 = bf16[8,4,64,12,64]{2,1,4,3,0:T(4,128)(2,1)} copy(bf16[8,4,64,12,64]{2,0,1,4,3:T(8,128)(2,1)} %bitcast.216) | data formatting | bytes 6291456 | tf_op jit(solution)/shard_map/transpose | solution.py:584
  313.5 10.2 %reshape.408 = bf16[8,256,12,64]{1,3,2,0:T(8,128)(2,1)} reshape(bf16[8,4,64,12,64]{2,1,4,3,0:T(4,128)(2,1)} %copy.59) | data formatting | bytes 6291456 | tf_op jit(solution)/shard_map/reshape | solution.py:585
  323.6 6.2 fusion.88
  340.5 19.8 %multiply_convert_fusion.2 = (bf16[512,3072]{1,0:T(8,128)(2,1)S(1)}, f32[512,3072]{1,0:T(8,128)S(1)}, f32[512,3072]{1,0:T(8,128)}) fusion(f32[3072]{0:T(1024)S(1)} %add.193, bf16[768,3072]{1,0:T(8,128)(2,1)} %copy-done.6, f32[512,768]{1,0:T(8,128)S(1)} %get-tuple-element.96, f32[768]{0:T(1024)S(1)} %add.190, f32[768]{0:T(1024)S(1)} %mul.281, ...), kind=kOutput, calls=%fused_computation.20 | convolution fusion | flops 2521694208 | bytes 22042624 | tf_op jit(solution)/shard_map/dot_general | solution.py:425
  360.4 8.2 %convert_reduce_fusion.1 = (f32[3072]{0:T(1024)S(1)}, bf16[512,3072]{1,0:T(8,128)(2,1)S(1)}) fusion(f32[512,3072]{1,0:T(8,128)S(1)} %get-tuple-element.69, bf16[512,768]{1,0:T(8,128)(2,1)S(1)} %bitcast.220, bf16[768,3072]{1,0:T(8,128)(2,1)S(1)} %bitcast.211, f32[512,3072]{1,0:T(8,128)} %get-tuple-element.97, f32[3072]{0:T(1024)S(1)} %add.193), kind=kOutput, calls=%fused_computation.17 | convolution fusion | flops 2442654720 | bytes 21258240 | tf_op jit(solution)/shard_map/dot_general | solution.py:425
  399.8 6.5 fusion.16.refs_4_
  406.3 5.6 convert_bitcast_fusion
  450.0 5.6 multiply_reduce_fusion.1
  509.4 12.8 %concatenate.31.refs_1_ = bf16[4,768,1152]{2,1,0:T(8,128)(2,1)} concatenate(bf16[4,768,576]{2,1,0:T(8,128)(2,1)} %bitcast.218, bf16[4,768,192]{2,1,0:T(8,128)(2,1)} %bitcast.225, bf16[4,768,192]{2,1,0:T(8,128)(2,1)} %bitcast.226, bf16[4,768,192]{2,1,0:T(8,128)(2,1)} %bitcast.224), dimensions={2} | concatenate | bytes 14155776 | tf_op jit(solution)/shard_map/concatenate | solution.py:694
  522.2 5.5 reshape.421
  527.8 8.3 %convert_reduce_fusion = f32[768]{0:T(1024)S(1)} fusion(bf16[8,4,64,768]{2,1,3,0:T(4,128)(2,1)} %reshape.421), kind=kLoop, calls=%fused_computation.2 | loop fusion | flops 3144960 | bytes 3148800 | tf_op jit(solution)/shard_map/reduce_sum | solution.py:441
  537.3 10.0 %copy.92 = bf16[4,8,64,768]{3,2,1,0:T(8,128)(2,1)} copy(bf16[4,8,64,768]{2,0,3,1:T(4,128)(2,1)} %bitcast.214) | data formatting | bytes 6291456 | tf_op jit(solution)/shard_map/transpose | solution.py:591
  552.6 10.1 %copy.91 = bf16[4,8,64,768]{3,2,1,0:T(8,128)(2,1)} copy(bf16[4,8,64,768]{2,0,3,1:T(4,128)(2,1)} %bitcast.217) | data formatting | bytes 6291456 | tf_op jit(solution)/shard_map/transpose | solution.py:591
  562.7 9.3 %fusion.20.refs_2_ = bf16[768,1536]{1,0:T(8,128)(2,1)} fusion(bf16[2048,768]{1,0:T(8,128)(2,1)S(1)} %bitcast.213, bf16[2048,768]{1,0:T(8,128)(2,1)} %bitcast.230, bf16[2048,768]{1,0:T(8,128)(2,1)} %bitcast.232), kind=kOutput, calls=%fused_computation.47 | convolution fusion | flops 4845600768 | bytes 11796480 | tf_op jit(solution)/shard_map/dot_general | solution.py:429
  572.1 6.4 fusion.21
  578.5 135.4 %shard_map.238 = (f32[16,128]{1,0:T(8,128)}, f32[96,1152]{1,0:T(8,128)}, f32[96,384]{1,0:T(8,128)}, f32[96,768]{1,0:T(8,128)}, f32[192,384]{1,0:T(8,128)}, /*index=5*/bf16[32,64,768]{2,1,0:T(8,128)(2,1)}) custom-call(f32[4,128,128]{2,1,0:T(8,128)} %broadcast_in_dim.102.refs_0_, bf16[4,768,1152]{2,1,0:T(8,128)(2,1)} %concatenate.31.refs_1_, ...), custom_call_target="tpu_custom_call" | custom-call | tf_op jit(solution)/shard_map/pallas_call | solution.py:387
  (344 shorter events, 240.7 us)
Async XLA Ops:
  0.6 9.5 %copy-start.4 = (bf16[384,192]{0,1:T(8,128)(2,1)S(1)}, bf16[384,192]{0,1:T(8,128)(2,1)}, u32[]{:S(2)}) copy-start(bf16[384,192]{0,1:T(8,128)(2,1)} %param.23) | copy-start | bytes 442372
  0.7 9.5 %copy-start.3 = (bf16[96,768]{1,0:T(8,128)(2,1)S(1)}, bf16[96,768]{1,0:T(8,128)(2,1)}, u32[]{:S(2)}) copy-start(bf16[96,768]{1,0:T(8,128)(2,1)} %refs_3_.1) | copy-start | bytes 442372
  0.7 9.3 %copy-start.57 = (bf16[96,192]{1,0:T(8,128)(2,1)S(1)}, bf16[96,192]{1,0:T(8,128)(2,1)}, u32[]{:S(2)}) copy-start(bf16[96,192]{1,0:T(8,128)(2,1)} %param.21) | copy-start | bytes 110596
  0.7 9.5 %copy-start.5 = (bf16[96,384]{1,0:T(8,128)(2,1)S(1)}, bf16[96,384]{1,0:T(8,128)(2,1)}, u32[]{:S(2)}) copy-start(bf16[96,384]{1,0:T(8,128)(2,1)} %refs_2_.1) | copy-start | bytes 221188
  0.7 9.3 %copy-start.56 = (bf16[96,192]{1,0:T(8,128)(2,1)S(1)}, bf16[96,192]{1,0:T(8,128)(2,1)}, u32[]{:S(2)}) copy-start(bf16[96,192]{1,0:T(8,128)(2,1)} %param.19) | copy-start | bytes 110596
  0.7 9.3 %copy-start.55 = (bf16[96,192]{1,0:T(8,128)(2,1)S(1)}, bf16[96,192]{1,0:T(8,128)(2,1)}, u32[]{:S(2)}) copy-start(bf16[96,192]{1,0:T(8,128)(2,1)} %param.18) | copy-start | bytes 110596
  0.7 9.3 %copy-start.50 = (bf16[96,576]{1,0:T(8,128)(2,1)S(1)}, bf16[96,576]{1,0:T(8,128)(2,1)}, u32[]{:S(2)}) copy-start(bf16[96,576]{1,0:T(8,128)(2,1)} %param.17) | copy-start | bytes 331780
  12.1 170.9 %copy-start.13 = (bf16[8,64,768]{2,1,0:T(8,128)(2,1)S(1)}, bf16[8,64,768]{2,1,0:T(8,128)(2,1)}, u32[]{:S(2)}) copy-start(bf16[8,64,768]{2,1,0:T(8,128)(2,1)} %param.14) | copy-start | bytes 2359300
  182.2 58.8 %copy-start.76 = (f32[768]{0:T(1024)}, f32[768]{0:T(1024)S(1)}, u32[]{:S(2)}) copy-start(f32[768]{0:T(1024)S(1)} %mul.274) | copy-start | bytes 9220
  182.5 58.6 %copy-start.81 = (f32[768]{0:T(1024)}, f32[768]{0:T(1024)S(1)}, u32[]{:S(2)}) copy-start(f32[768]{0:T(1024)S(1)} %add.179) | copy-start | bytes 9220
  288.8 34.8 %copy-start.17 = (bf16[8,256,12,64]{1,3,2,0:T(8,128)(2,1)}, bf16[8,256,12,64]{1,3,2,0:T(8,128)(2,1)S(1)}, u32[]{:S(2)}) copy-start(bf16[8,256,12,64]{1,3,2,0:T(8,128)(2,1)S(1)} %reshape.412) | copy-start | bytes 9437188
  337.6 22.7 %slice-start.2 = ((s8[4718592]{0:T(1024)(128)(4,1)}), s8[4194304]{0:T(1024)(128)(4,1)S(1)}, s32[]{:S(2)}) async-start(s8[4718592]{0:T(1024)(128)(4,1)} %bitcast.210), calls=%async_computation.2 | async-start | bytes 8388608
  337.6 34.6 %slice-start = ((s8[4718592]{0:T(1024)(128)(4,1)}), s8[4194304]{0:T(1024)(128)(4,1)S(1)}, s32[]{:S(2)}) async-start(s8[4718592]{0:T(1024)(128)(4,1)} %bitcast.208), calls=%async_computation | async-start | bytes 8388608
  340.2 32.0 %copy-start.26 = (f32[512,768]{1,0:T(8,128)}, f32[512,768]{1,0:T(8,128)S(1)}, u32[]{:S(2)}) copy-start(f32[512,768]{1,0:T(8,128)S(1)} %get-tuple-element.96) | copy-start | bytes 4718596
  340.5 19.8 %slice-start.3 = ((s8[4718592]{0:T(1024)(128)(4,1)}), s8[524288]{0:T(1024)(128)(4,1)S(1)}, s32[]{:S(2)}) async-start(s8[4718592]{0:T(1024)(128)(4,1)} %bitcast.210), calls=%async_computation.3 | async-start | bytes 1048576
  340.5 19.8 %copy-start.20 = (bf16[8,64,768]{2,1,0:T(8,128)(2,1)S(1)}, bf16[8,64,768]{2,1,0:T(8,128)(2,1)}, u32[]{:S(2)}) copy-start(bf16[8,64,768]{2,1,0:T(8,128)(2,1)} %param.27) | copy-start | bytes 2359300
  340.5 31.6 %slice-start.1 = ((s8[4718592]{0:T(1024)(128)(4,1)}), s8[524288]{0:T(1024)(128)(4,1)S(1)}, s32[]{:S(2)}) async-start(s8[4718592]{0:T(1024)(128)(4,1)} %bitcast.208), calls=%async_computation.1 | async-start | bytes 1048576
  399.8 12.2 %slice-start.4 = ((s8[6291456]{0:T(1024)(128)(4,1)}), s8[4194304]{0:T(1024)(128)(4,1)S(1)}, s32[]{:S(2)}) async-start(s8[6291456]{0:T(1024)(128)(4,1)} %bitcast.222), calls=%async_computation.4 | async-start | bytes 8388608
  509.4 12.8 %copy-start.35 = (bf16[8,256,12,64]{1,3,2,0:T(8,128)(2,1)S(1)}, bf16[8,256,12,64]{1,3,2,0:T(8,128)(2,1)}, u32[]{:S(2)}) copy-start(bf16[8,256,12,64]{1,3,2,0:T(8,128)(2,1)} %convert_bitcast_fusion) | copy-start | bytes 9437188
  537.3 10.0 %copy-start.19 = (bf16[8,256,12,64]{1,3,2,0:T(8,128)(2,1)S(1)}, bf16[8,256,12,64]{1,3,2,0:T(8,128)(2,1)}, u32[]{:S(2)}) copy-start(bf16[8,256,12,64]{1,3,2,0:T(8,128)(2,1)} %fusion.22) | copy-start | bytes 9437188
  552.6 10.1 %copy-start.10 = (bf16[4,8,64,768]{3,2,1,0:T(8,128)(2,1)S(1)}, bf16[4,8,64,768]{3,2,1,0:T(8,128)(2,1)}, u32[]{:S(2)}) copy-start(bf16[4,8,64,768]{3,2,1,0:T(8,128)(2,1)} %copy-done.8) | copy-start | bytes 9437188
  562.7 9.4 %copy-start.12 = (bf16[768,1536]{1,0:T(8,128)(2,1)S(1)}, bf16[768,1536]{1,0:T(8,128)(2,1)}, u32[]{:S(2)}) copy-start(bf16[768,1536]{1,0:T(8,128)(2,1)} %copy-done.11) | copy-start | bytes 7077892
  562.7 9.4 %copy-start.37 = (bf16[4,8,64,768]{3,2,1,0:T(8,128)(2,1)S(1)}, bf16[4,8,64,768]{3,2,1,0:T(8,128)(2,1)}, u32[]{:S(2)}) copy-start(bf16[4,8,64,768]{3,2,1,0:T(8,128)(2,1)} %copy.92) | copy-start | bytes 9437188
  562.7 9.4 %copy-start.38 = (bf16[4,8,64,768]{3,2,1,0:T(8,128)(2,1)S(1)}, bf16[4,8,64,768]{3,2,1,0:T(8,128)(2,1)}, u32[]{:S(2)}) copy-start(bf16[4,8,64,768]{3,2,1,0:T(8,128)(2,1)} %copy.91) | copy-start | bytes 9437188
  (68 other events, 293.1 us)
